TPU v7x, 32 devices: a whole 2x2x4 slice. The times are simulated.
32 devices in a mesh: blk: 8 (over y, x, core), walk: 4 (over z).
Axes of the slice: x: 2, y: 2, z: 4, core: 2. Of those that a mesh axis runs over, the one named last changes fastest.
Arguments:
- walkers: bfloat16 [64, 200, 2048], P(('blk', 'walk')), may hold values from -6 to 6
- inv_intersection: bfloat16 [64, 2, 100, 100], P(('blk', 'walk')), may hold values from -0.625 to 0.625
- rotated_chol: bfloat16 [16, 100, 2048], P('blk'), may hold values from -0.013671875 to 0.013671875
- full_chol: bfloat16 [16, 2048, 2048], P('walk', 'blk'), may hold values from -0.125 to 0.125
- field_noise: float32 [16], replicated, may hold values from -4 to 4
Outputs:
- propagated: bfloat16 [64, 200, 2048], P(('blk', 'walk'))
- force_bias: float32 [64, 16], P(('blk', 'walk'))
- bias_shift: float32 [16], replicated
All inputs are finite; a program needn't handle non-finite values.
Results may differ from a plain program's by a relative error of at most 0.0065.
Values may be sent and summed in bfloat16 or wider, within the bound.
A program may use at most 128 MiB of HBM per device.

v0:
```python
import math

import jax
import jax.numpy as jnp
from jax import lax
from jax.sharding import PartitionSpec as P

time_root = 0.1


def local(walkers, inv_intersection, rotated_chol, full_chol, field_noise):
    wdev_count, double_rows, orbitals = walkers.shape
    occupied = double_rows // 2
    spins = walkers.reshape(wdev_count, 2, occupied, orbitals)
    theta = jnp.einsum(
        "wsij,wsjp->wip", inv_intersection, spins, preferred_element_type=jnp.float32
    ).astype(jnp.bfloat16)
    flat_theta = theta.reshape(wdev_count, occupied * orbitals)
    piece = lax.all_gather(rotated_chol, "blk", axis=0, tiled=True)
    flat_piece = piece.reshape(piece.shape[0], occupied * orbitals)
    part_bias = lax.dot_general(
        flat_theta, flat_piece, (((1,), (1,)), ((), ())), preferred_element_type=jnp.float32
    )
    total_walkers = wdev_count * lax.axis_size("blk") * lax.axis_size("walk")
    bias_shift = lax.psum(jnp.sum(part_bias, axis=0), ("blk", "walk")) / math.sqrt(total_walkers)
    shifted = field_noise - bias_shift
    local_count = full_chol.shape[0]
    local_shift = lax.dynamic_slice_in_dim(
        shifted, lax.axis_index("walk") * local_count, local_count
    )
    partial_value = time_root * jnp.tensordot(
        local_shift, full_chol.astype(jnp.float32), axes=1, precision=lax.Precision.HIGHEST
    )
    row_block = lax.psum(partial_value, "walk").astype(jnp.bfloat16)
    field = lax.all_gather(row_block, "blk", axis=0, tiled=True)
    current = walkers.reshape(wdev_count * double_rows, orbitals)
    total = current.astype(jnp.float32)
    for order in range(1, 5):
        current = (jnp.dot(current, field, preferred_element_type=jnp.float32) / order).astype(
            jnp.bfloat16
        )
        total = total + current.astype(jnp.float32)
    propagated = total.astype(jnp.bfloat16).reshape(wdev_count, double_rows, orbitals)
    return (propagated, part_bias, bias_shift)


def solution(mesh):
    placed = (
        P(("blk", "walk"), None, None),
        P(("blk", "walk"), None, None, None),
        P("blk", None, None),
        P("walk", "blk", None),
        P(),
    )
    return jax.shard_map(
        local,
        mesh=mesh,
        in_specs=placed,
        out_specs=(P(("blk", "walk"), None, None), P(("blk", "walk"), None), P()),
        check_vma=False,
    )
```

profile of v0, /device:TPU:1, one launch (start us, length us, event | category | flops | bytes accessed | tf_op | source)
XLA Modules:
  0.0 281.4 jit_solution(11775404519253080099)
XLA Ops:
  7.2 0.0 copy-start
  7.2 0.0 copy-start.2
  7.2 0.0 all-gather.3.cloned.1.call-start
  7.2 2.4 copy.9
  9.7 0.0 all-gather.3.cloned.1.call-update
  9.7 0.0 all-gather.5.cloned.1.call-start
  9.7 0.0 copy-done
  9.7 0.4 reshape.18
  10.1 0.0 copy-done.2
  10.1 0.4 fusion.8
  10.6 0.0 copy-start.3
  10.6 50.0 %all-gather.3.cloned.1.call-done = bf16[16,100,2048]{2,1,0:T(8,128)(2,1)} async-done(((bf16[2,100,2048]{2,1,0:T(8,128)(2,1)}), bf16[16,100,2048]{2,1,0:T(8,128)(2,1)}) %all-gather.3.cloned.1.call-update) | async-done | bytes 6553616 | tf_op jit(solution)/shard_map/all_gather | solution.py:19
  60.6 13.2 %fusion.15 = (f32[16]{0:T(128)S(1)}, f32[2,16]{1,0:T(2,128)}) fusion(bf16[16,100,2048]{2,1,0:T(8,128)(2,1)} %all-gather.3.cloned.1.call-done, bf16[2,100,2048]{2,1,0:T(8,128)(2,1)S(1)} %fusion.8), kind=kOutput, calls=%fused_computation.22 | convolution fusion | flops 13107216 | bytes 7372992 | tf_op jit(solution)/shard_map/dot_general | solution.py:21
  73.7 38.2 %psum.14 = f32[16]{0:T(128)S(1)} all-reduce(f32[16]{0:T(128)S(1)} %get-tuple-element.5), channel_id=1, replica_groups=mesh['blk'=8,'walk'=4] {'blk','walk'}, use_global_device_ids=true, to_apply=%region_1.0 | all-reduce | flops 16 | bytes 128 | tf_op jit(solution)/shard_map/psum | solution.py:25
  111.9 0.0 copy-done.3
  111.9 0.5 fusion.14
  112.4 10.6 %fusion.2 = f32[1,256,2048]{2,0,1:T(1,128)S(1)} fusion(bf16[4,256,2048]{2,1,0:T(8,128)(2,1)} %param.8, f32[16]{0:T(128)S(1)} %get-tuple-element.3, s32[]{:T(128)S(6)} %select_n.3), kind=kOutput, calls=%fused_computation.2 | convolution fusion | flops 25165824 | bytes 6291524 | tf_op jit(solution)/shard_map/dot_general | solution.py:31
  123.1 1.0 bitcast_multiply_fusion
  124.1 72.0 %all-reduce.1 = bf16[256,2048]{1,0:T(8,128)(2,1)} all-reduce(f32[256,2048]{1,0:T(8,128)S(1)} %bitcast_multiply_fusion), channel_id=1, replica_groups=mesh['blk'=8,'walk'=4] {'walk'}, use_global_device_ids=true, to_apply=%region_2.0 | all-reduce | flops 524288 | bytes 3145728 | tf_op jit(solution)/shard_map/psum | solution.py:34
  196.0 0.0 all-gather.5.cloned.1.call-update
  196.0 58.6 %all-gather.5.cloned.1.call-done = bf16[2048,2048]{1,0:T(8,128)(2,1)} async-done(((bf16[256,2048]{1,0:T(8,128)(2,1)}), bf16[2048,2048]{1,0:T(8,128)(2,1)}) %all-gather.5.cloned.1.call-update) | async-done | bytes 8388624 | tf_op jit(solution)/shard_map/all_gather | solution.py:35
  254.7 0.0 copy-start.4
  254.7 7.6 %convolution_convert_fusion = bf16[2048,400]{0,1:T(8,128)(2,1)S(1)} fusion(bf16[400,2048]{1,0:T(8,128)(2,1)} %bitcast.33, bf16[2048,2048]{1,0:T(8,128)(2,1)} %all-gather.5.cloned.1.call-done), kind=kOutput, calls=%fused_computation.12 | convolution fusion | flops 3356262400 | bytes 11665408 | tf_op jit(solution)/shard_map/dot_general | solution.py:39
  262.2 0.0 copy-done.4
  262.2 3.6 %multiply_convert_fusion.2 = bf16[400,2048]{1,0:T(8,128)(2,1)S(1)} fusion(bf16[2048,400]{0,1:T(8,128)(2,1)S(1)} %convolution_convert_fusion, bf16[2048,2048]{1,0:T(8,128)(2,1)S(1)} %copy-done.4), kind=kOutput, calls=%fused_computation.11 | convolution fusion | flops 3357081600 | bytes 11665408 | tf_op jit(solution)/shard_map/dot_general | solution.py:39
  265.9 0.0 copy-start.1
  265.9 3.6 %multiply_convert_fusion.1 = bf16[400,2048]{1,0:T(8,128)(2,1)S(1)} fusion(bf16[400,2048]{1,0:T(8,128)(2,1)S(1)} %multiply_convert_fusion.2, bf16[2048,2048]{1,0:T(8,128)(2,1)S(1)} %copy-done.4), kind=kOutput, calls=%fused_computation.10 | convolution fusion | flops 3357081600 | bytes 11665408 | tf_op jit(solution)/shard_map/dot_general | solution.py:39
  269.5 0.0 copy-done.1
  269.5 5.1 %fusion.7 = bf16[400,2048]{1,0:T(8,128)(2,1)} fusion(bf16[2048,400]{0,1:T(8,128)(2,1)S(1)} %convolution_convert_fusion, bf16[400,2048]{1,0:T(8,128)(2,1)S(1)} %multiply_convert_fusion.1, bf16[400,2048]{1,0:T(8,128)(2,1)S(1)} %multiply_convert_fusion.2, bf16[400,2048]{1,0:T(8,128)(2,1)S(1)} %bitcast.34, bf16[2048,2048]{1,0:T(8,128)(2,1)S(1)} %copy-done.4), kind=kOutput, calls=%fused_computation.8 | convolution fusion | flops 3365273600 | bytes 16580608 | tf_op jit(solution)/shard_map/dot_general | solution.py:39
Async XLA Ops:
  7.2 2.6 copy-start
  7.2 3.0 %copy-start.2 = (bf16[2,2,100,100]{3,1,2,0:T(2,128)(2,1)S(1)}, bf16[2,2,100,100]{3,1,2,0:T(2,128)(2,1)}, u32[]{:S(2)}) copy-start(bf16[2,2,100,100]{3,1,2,0:T(2,128)(2,1)} %param.6) | copy-start | bytes 240004
  7.2 53.4 %all-gather.3.cloned.1.call-start = ((), (), s32[]{:S(2)}) async-start(), calls=%async_computation | async-start | bytes 7667712 | tf_op jit(solution)/shard_map/all_gather | solution.py:19
  9.7 245.0 %all-gather.5.cloned.1.call-start = ((), (), s32[]{:S(2)}) async-start(), calls=%async_computation.1 | async-start | bytes 9437184 | tf_op jit(solution)/shard_map/all_gather | solution.py:35
  10.6 101.4 %copy-start.3 = (f32[16]{0:T(128)S(1)}, f32[16]{0:T(128)}, u32[]{:S(2)}) copy-start(f32[16]{0:T(128)} %param.9) | copy-start | bytes 196
  254.7 7.6 %copy-start.4 = (bf16[2048,2048]{1,0:T(8,128)(2,1)S(1)}, bf16[2048,2048]{1,0:T(8,128)(2,1)}, u32[]{:S(2)}) copy-start(bf16[2048,2048]{1,0:T(8,128)(2,1)} %all-gather.5.cloned.1.call-done) | copy-start | bytes 25165828
  265.9 3.6 %copy-start.1 = (bf16[2,200,2048]{2,1,0:T(8,128)(2,1)S(1)}, bf16[2,200,2048]{2,1,0:T(8,128)(2,1)}, u32[]{:S(2)}) copy-start(bf16[2,200,2048]{2,1,0:T(8,128)(2,1)} %param.5) | copy-start | bytes 4915204
Sparse Core Ops, SparseCore 0:
  10.5 50.0 all-gather.2
  196.2 58.4 all-gather.4
where the time goes:
time: 282 us; the launch traced here: 281 us
  blocking collectives  110 us (39%)
  waiting for transfers between devices  109 us (39%)
  matrix products  44.1 us (16%)
  between operations  14.2 us (5%)
  local copies, waits for them, and re-layouts  2.83 us (1%)
    psum x1, blocking collectives, local(): row_block = lax.psum(partial_value, 'walk').astype(jnp.bfloat16)  72 us
    all_gather x1, waiting for transfers between devices, local(): field = lax.all_gather(row_block, 'blk', axis=0, tiled=True)  58.6 us
    all_gather x1, waiting for transfers between devices, local(): piece = lax.all_gather(rotated_chol, 'blk', axis=0, tiled=True)  50 us
    psum x1, blocking collectives, local(): lax.psum(jnp.sum(part_bias, axis=0), ('blk', 'walk'))  38.2 us
    dot_general x4, matrix products, local(): jnp.dot(current, field, preferred_element_type=jnp.float32) / order  19.9 us
    dot_general x1, matrix products, local(): lax.dot_general(flat_theta, flat_piece, (((1,), (1,)), ((), ())), preferr...  13.2 us
    dot_general x1, matrix products, local(): jnp.tensordot(local_shift, full_chol.astype(jnp.float32), axes=1, precisi...  10.6 us
  transfers between devices with their start and end apart: 2, of which 2 were waited for; matrix products, arithmetic and copies ran while one was open for 0% of the time, Pallas kernels for 0%

commit v1 on v0

v1 whole, which is shorter than its diff:
```python
import functools
import math

import jax
import jax.numpy as jnp
from jax import lax
from jax.experimental import pallas as pl
from jax.experimental.pallas import tpu as pltpu
from jax.sharding import PartitionSpec as P

time_root = 0.1
orders = 4
f32, bf16 = jnp.float32, jnp.bfloat16


class Gather:
    def __init__(self, nb, chunks, ref_at, many, recv, send_f, send_s, send_b):
        self.nb, self.chunks, self.ref_at, self.many = nb, chunks, ref_at, many
        self.recv, self.send_f, self.send_s, self.send_b = recv, send_f, send_s, send_b
        me = lax.axis_index("blk")
        self.me, self.core = me, me % 2
        self.cols = 2 if nb % 4 == 0 else 1
        self.rows = nb // 2 // self.cols
        chip = me // 2
        col, row = chip % self.cols, chip // self.cols
        self.turn = self.core if self.rows == self.cols else 0
        self.f = (1 - self.turn) * col + self.turn * row
        self.s = (1 - self.turn) * row + self.turn * col
        self.nf, self.ns = self.cols, self.rows
        self.sibling = chip * 2 + 1 - self.core

    def at(self, i, j, core=None):
        f, s = (self.f + i) % self.nf, (self.s + j) % self.ns
        chip = (1 - self.turn) * (s * self.cols + f) + self.turn * (f * self.cols + s)
        return chip * 2 + (self.core if core is None else core)

    def copy(self, block, chunk, target, send):
        piece = self.ref_at(block, chunk)
        return pltpu.make_async_remote_copy(
            src_ref=piece, dst_ref=piece, send_sem=send, recv_sem=self.recv.at[block, chunk],
            device_id={"blk": target}, device_id_type=pl.DeviceIdType.MESH)

    def landed(self, block, chunk):
        self.copy(block, chunk, self.sibling, self.send_b).wait_recv()

    def own(self, chunk):
        for i in range(1, self.nf):
            self.copy(self.me, chunk, self.at(i, 0), self.send_f).start()
        for j in range(1, self.ns):
            self.copy(self.me, chunk, self.at(0, j), self.send_s).start()
        self.copy(self.me, chunk, self.sibling, self.send_b).start()

    def first(self, chunk):
        for i in range(1, self.nf):
            block = self.at(i, 0)
            self.landed(block, chunk)
            for j in range(1, self.ns):
                self.copy(block, chunk, self.at(0, j), self.send_s).start()
            self.copy(block, chunk, self.sibling, self.send_b).start()

    def second(self, chunk):
        for j in range(1, self.ns):
            for i in range(self.nf):
                block = self.at(i, j)
                self.landed(block, chunk)
                self.copy(block, chunk, self.sibling, self.send_b).start()

    def drain(self):
        for send, count in ((self.send_f, self.nf - 1), (self.send_s, (self.ns - 1) * self.nf), (self.send_b, self.nb // 2)):
            if count:
                piece = self.many(count)
                pltpu.make_async_remote_copy(
                    src_ref=piece, dst_ref=piece, send_sem=send, recv_sem=self.recv.at[0, 0],
                    device_id={"blk": self.sibling}, device_id_type=pl.DeviceIdType.MESH).wait_send()


def kernel(nb, nw, total_walkers, chunks, flat, three, inv, rot_hbm, full_hbm, noise,
           out, fb, shift,
           rot, full, theta, acc, field, mid, outer_in, inner_in, slots_w, slots_b, current, total,
           rot_recv, rot_f, rot_s, rot_b, fld_recv, fld_f, fld_s, fld_b,
           load, slot_send, slot_recv, in_send, in_recv, mid_send, mid_recv, out_send, out_recv):
    blk, walk = lax.axis_index("blk"), lax.axis_index("walk")
    wdev, occupied, orbitals = theta.shape
    per, group = rot_hbm.shape[0], rot.shape[0]
    local_count, block_rows = full_hbm.shape[0], full_hbm.shape[1]
    size = block_rows // chunks
    MESH = pl.DeviceIdType.MESH

    load_rot = pltpu.make_async_copy(rot_hbm, rot.at[pl.ds(blk * per, per)], load.at[0])
    load_rot.start()
    load_full = pltpu.make_async_copy(full_hbm, full, load.at[1])
    load_full.start()
    barrier = pltpu.get_barrier_semaphore()
    for d in range(1, nb):
        pl.semaphore_signal(barrier, inc=1, device_id={"blk": (blk + d) % nb}, device_id_type=MESH)
    for d in range(1, nw):
        pl.semaphore_signal(barrier, inc=1, device_id={"walk": (walk + d) % nw}, device_id_type=MESH)
    pl.semaphore_wait(barrier, nb + nw - 2)
    load_rot.wait()

    vectors = Gather(nb, per, lambda block, c: rot.at[block * per + c], lambda k: rot.at[pl.ds(0, k * per)],
                     rot_recv, rot_f, rot_s, rot_b)
    for c in range(per):
        vectors.own(c)

    tile = 512
    for w in range(wdev):
        for lo in range(0, orbitals, tile):
            theta[w, :, lo:lo + tile] = jnp.dot(inv[w], three[w, :, lo:lo + tile], preferred_element_type=f32).astype(bf16)

    def bias(g):
        for lo in range(0, orbitals, 256):
            vector = rot[g, :, lo:lo + 256].astype(f32)
            for w in range(wdev):
                product = vector * theta[w, :, lo:lo + 256].astype(f32)
                acc[pl.ds(w * group + g, 1), lo:lo + 256] = jnp.sum(product, axis=0, keepdims=True)

    def bias_block(block):
        @pl.loop(0, per)
        def _(c):
            bias(block * per + c)

    bias_block(blk)
    for c in range(per):
        vectors.first(c)
    for i in range(1, vectors.nf):
        bias_block(vectors.at(i, 0))
    for c in range(per):
        vectors.landed(vectors.sibling, c)
    bias_block(vectors.sibling)
    for c in range(per):
        vectors.second(c)
    for j in range(1, vectors.ns):
        for i in range(vectors.nf):
            bias_block(vectors.at(i, j))

    @pl.loop(1, nb // 2)
    def _(d):
        block = (vectors.sibling + 2 * d) % nb
        for c in range(per):
            vectors.landed(block, c)
        bias_block(block)

    biases = jnp.sum(acc[...], axis=1, keepdims=True)
    fb[...] = jnp.broadcast_to(biases, fb.shape)
    part = biases[0:group]
    for w in range(1, wdev):
        part = part + biases[w * group:(w + 1) * group]
    diagonal = lax.broadcasted_iota(jnp.int32, (group, 128), 0) == lax.broadcasted_iota(jnp.int32, (group, 128), 1)
    line = jnp.sum(jnp.where(diagonal, jnp.broadcast_to(part, (group, 128)), 0.0), axis=0, keepdims=True)
    for axis, count, me, slots, k in (("walk", nw, walk, slots_w, 0), ("blk", nb, blk, slots_b, 1)):
        slots[pl.ds(me, 1)] = line[None]
        if count > 1:
            for d in range(1, count):
                pltpu.make_async_remote_copy(
                    src_ref=slots.at[me], dst_ref=slots.at[me], send_sem=slot_send.at[k], recv_sem=slot_recv.at[k],
                    device_id={axis: (me + d) % count}, device_id_type=MESH).start()
            rest = slots.at[pl.ds(0, count - 1)]
            every = pltpu.make_async_remote_copy(
                src_ref=rest, dst_ref=rest, send_sem=slot_send.at[k], recv_sem=slot_recv.at[k],
                device_id={axis: (me + 1) % count}, device_id_type=MESH)
            every.wait()
        line = slots[0]
        for d in range(1, count):
            line = line + slots[d]
    shifts = line / math.sqrt(total_walkers)
    shift[...] = shifts
    shifted = (noise[...] - shifts[:, 0:group]) * time_root
    lane = lax.broadcasted_iota(jnp.int32, (1, group), 1)
    weights = [jnp.sum(jnp.where(lane == walk * local_count + j, shifted, 0.0), axis=1, keepdims=True)
               for j in range(local_count)]
    load_full.wait()

    half = nw // 2
    low = walk < half
    is_mid = (walk == half - 1) | (walk == half)
    has_outer = (walk != 0) & (walk != nw - 1)
    step = 1 - 2 * (walk >= half).astype(jnp.int32)
    inward = (walk + step + nw) % nw
    outward = (walk - step + nw) % nw
    lag = jnp.where(is_mid, 1, 3)
    rows = lambda block, c: field.at[pl.ds(pl.multiple_of(block * block_rows + c * size, size), size)]
    gather = Gather(nb, chunks, rows, lambda k: field.at[pl.ds(0, k * block_rows)], fld_recv, fld_f, fld_s, fld_b)

    def hop(src, dst, send, recv, target):
        return pltpu.make_async_remote_copy(src_ref=src, dst_ref=dst, send_sem=send, recv_sem=recv,
                                            device_id={"walk": target}, device_id_type=MESH)

    def to_mid(c):
        return hop(mid.at[c], outer_in.at[c], in_send.at[c], in_recv.at[c], inward)

    def across(c):
        return hop(mid.at[c], inner_in.at[c], mid_send.at[c], mid_recv.at[c], inward)

    def back(c):
        return hop(rows(blk, c), rows(blk, c), out_send.at[c], out_recv.at[c], outward)

    def reduce_in(c):
        span = pl.ds(pl.multiple_of(c * size, size), size)

        def summed():
            value = weights[0] * full[0, span, :].astype(f32)
            for j in range(1, local_count):
                value = value + weights[j] * full[j, span, :].astype(f32)
            return value

        @pl.when(has_outer)
        def _():
            to_mid(c).wait_recv()
            mid[c] = (summed() + outer_in[c].astype(f32)).astype(bf16)

        @pl.when(jnp.logical_not(has_outer))
        def _():
            mid[c] = summed().astype(bf16)

        @pl.when(is_mid)
        def _():
            across(c).start()

        @pl.when(jnp.logical_not(is_mid))
        def _():
            to_mid(c).start()

    def spread(c):
        @pl.when(is_mid)
        def _():
            across(c).wait_recv()
            span = pl.ds(pl.multiple_of(blk * block_rows + c * size, size), size)
            field[span, :] = (mid[c].astype(f32) + inner_in[c].astype(f32)).astype(bf16)

        @pl.when(jnp.logical_not(is_mid))
        def _():
            back(c).wait_recv()

        @pl.when(has_outer)
        def _():
            back(c).start()

        gather.own(c)

    def when_chunk(c, action):
        @pl.when((c >= 0) & (c < chunks))
        def _():
            action(c)

    @pl.loop(0, chunks + 5)
    def _(t):
        when_chunk(t, reduce_in)
        when_chunk(t - lag, spread)
        when_chunk(t - lag - 1, gather.first)
        when_chunk(t - lag - 2, gather.second)

    @pl.loop(0, nb // 2)
    def _(d):
        @pl.loop(0, chunks)
        def _(c):
            gather.landed((gather.sibling + 2 * d) % nb, c)

    source = flat
    for order in range(1, orders + 1):
        target = current.at[order % 2]

        @pl.loop(0, orbitals // tile)
        def _(n):
            span = pl.ds(pl.multiple_of(n * tile, tile), tile)
            term = (jnp.dot(source[...], field[:, span], preferred_element_type=f32) / order).astype(bf16)
            before = flat[:, span].astype(f32) if order == 1 else total[:, span]
            after = before + term.astype(f32)
            if order == orders:
                out[:, span] = after.astype(bf16)
            else:
                target[:, span] = term
                total[:, span] = after

        source = target

    vectors.drain()
    gather.drain()

    @pl.loop(0, chunks)
    def _(c):
        @pl.when(is_mid)
        def _():
            across(c).wait_send()

        @pl.when(jnp.logical_not(is_mid))
        def _():
            to_mid(c).wait_send()

        @pl.when(has_outer)
        def _():
            back(c).wait_send()


def local(nb, nw, walkers, inv_intersection, rotated_chol, full_chol, field_noise):
    wdev, double_rows, orbitals = walkers.shape
    occupied = double_rows // 2
    group = field_noise.shape[0]
    per = rotated_chol.shape[0]
    local_count, block_rows, _ = full_chol.shape
    chunks = 8
    size = block_rows // chunks
    flat = walkers.reshape(wdev * double_rows, orbitals)
    inv = inv_intersection.transpose(0, 2, 1, 3).reshape(wdev, occupied, double_rows)
    vmem, hbm = pl.BlockSpec(memory_space=pltpu.VMEM), pl.BlockSpec(memory_space=pl.ANY)
    dma = pltpu.SemaphoreType.DMA
    out, fb, shift = pl.pallas_call(
        functools.partial(kernel, nb, nw, wdev * nb * nw, chunks),
        out_shape=(jax.ShapeDtypeStruct(flat.shape, bf16), jax.ShapeDtypeStruct((wdev * group, 128), f32),
                   jax.ShapeDtypeStruct((1, 128), f32)),
        in_specs=[vmem, vmem, vmem, hbm, hbm, vmem],
        out_specs=(vmem, vmem, vmem),
        scratch_shapes=[
            pltpu.VMEM((group, occupied, orbitals), bf16),
            pltpu.VMEM(full_chol.shape, bf16),
            pltpu.VMEM((wdev, occupied, orbitals), bf16),
            pltpu.VMEM((wdev * group, orbitals), f32),
            pltpu.VMEM((orbitals, orbitals), bf16),
            pltpu.VMEM((chunks, size, orbitals), bf16),
            pltpu.VMEM((chunks, size, orbitals), bf16),
            pltpu.VMEM((chunks, size, orbitals), bf16),
            pltpu.VMEM((nw, 1, 128), f32),
            pltpu.VMEM((nb, 1, 128), f32),
            pltpu.VMEM((2,) + flat.shape, bf16),
            pltpu.VMEM(flat.shape, f32),
            dma((nb, per)), dma, dma, dma,
            dma((nb, chunks)), dma, dma, dma,
            dma((2,)), dma((2,)), dma((2,)),
            dma((chunks,)), dma((chunks,)), dma((chunks,)), dma((chunks,)), dma((chunks,)), dma((chunks,)),
        ],
        compiler_params=pltpu.CompilerParams(collective_id=0, has_side_effects=True, vmem_limit_bytes=60 * 2**20),
    )(flat, walkers, inv, rotated_chol, full_chol, field_noise.reshape(1, group))
    return (out.reshape(walkers.shape), fb[:, 0].reshape(wdev, group), shift[0, :group])


def solution(mesh):
    placed = (
        P(("blk", "walk"), None, None),
        P(("blk", "walk"), None, None, None),
        P("blk", None, None),
        P("walk", "blk", None),
        P(),
    )
    return jax.shard_map(
        functools.partial(local, mesh.shape["blk"], mesh.shape["walk"]),
        mesh=mesh,
        in_specs=placed,
        out_specs=(P(("blk", "walk"), None, None), P(("blk", "walk"), None), P()),
        check_vma=False,
    )
```

time: 282 us -> 127 us (0.45)
  Pallas kernels: 0 us -> 117 us
  blocking collectives: 110 us -> 0 us
  waiting for transfers between devices: 109 us -> 0 us
  matrix products: 44.1 us -> 0 us
  between operations: 14.2 us -> 0.64 us
  local copies, waits for them, and re-layouts: 2.83 us -> 9.36 us
    pallas_call x0 -> x1, Pallas kernels: none -> 117 us  [local(): pl.pallas_call(functools.partial(kernel, nb, nw, wdev * nb * nw, chunks),...]
    psum x2 -> x0, blocking collectives: 110 us -> none  [the longest x1 72 us: local(): row_block = lax.psum(partial_value, 'walk').astype(jnp.bfloat16)]
    all_gather x2 -> x0, waiting for transfers between devices: 109 us -> none  [the longest x1 58.6 us: local(): field = lax.all_gather(row_block, 'blk', axis=0, tiled=True)]
    dot_general x7 -> x0, matrix products: 44.1 us -> none  [the longest x4 19.9 us: local(): jnp.dot(current, field, preferred_element_type=jnp.float32) / order]
  transfers between devices with their start and end apart: 2 -> 0, of which waited for: 2 -> 0; matrix products, arithmetic and copies ran while one was open for 0% -> 0% of each run, Pallas kernels for 0% -> 0%
where the time goes in v1:
time: 127 us
  Pallas kernels  117 us (92%)
  local copies, waits for them, and re-layouts  9.36 us (7%)
    pallas_call x1, Pallas kernels, local(): pl.pallas_call(functools.partial(kernel, nb, nw, wdev * nb * nw, chunks),...  117 us
    unnamed x2, local copies, waits for them, and re-layouts  5.09 us

profile of v1, /device:TPU:1, one launch (start us, length us, event | category | flops | bytes accessed | tf_op | source)
XLA Modules:
  0.0 126.8 jit_solution(12175744623261631969)
XLA Ops:
  0.6 1.7 %reshape.22.inv = bf16[2,100,200]{2,1,0:T(8,128)(2,1)} reshape(bf16[2,100,2,100]{3,2,1,0:T(2,128)(2,1)} %bitcast.8) | data formatting | bytes 160000 | tf_op jit(solution)/shard_map/reshape | solution.py:304
  2.3 2.3 %copy.11.rot_hbm = bf16[2,100,2048]{2,1,0:T(8,128)(2,1)} copy(bf16[2,100,2048]{2,0,1:T(2,128)(2,1)} %param.7) | data formatting | bytes 1638400 | tf_op args[2]
  4.6 116.8 %shard_map.76 = (bf16[400,2048]{1,0:T(8,128)(2,1)}, f32[32,128]{1,0:T(8,128)}, f32[1,128]{1,0:T(1,128)}) custom-call(bf16[400,2048]{1,0:T(8,128)(2,1)} %bitcast.6, bf16[2,200,2048]{2,1,0:T(8,128)(2,1)} %three.1, bf16[2,100,200]{2,1,0:T(8,128)(2,1)} %reshape.22.inv, bf16[2,100,2048]{2,1,0:T(8,128)(2,1)} %copy.11.rot_hbm, bf16[4,256,2048]{2,1,0:T(8,128)(2,1)} %full_hbm.1, ...), custom_call_target="tpu_custom_call" | custom-call | tf_op jit(solution)/shard_map/pallas_call | solution.py:307
  121.4 0.8 slice_reduce_fusion
  122.2 0.7 reshape_squeeze.3
  122.9 1.1 slice_bitcast_fusion
  124.0 2.8 %copy.14 = bf16[2,200,2048]{2,1,0:T(8,128)(2,1)} copy(bf16[2,200,2048]{2,1,0:T(8,128)(2,1)} %bitcast.7) | data formatting | bytes 3276800

commit v2 on v1

--- a/solution.py
+++ b/solution.py
@@ -44,10 +44,16 @@
         self.copy(block, chunk, self.sibling, self.send_b).wait_recv()
 
     def own(self, chunk):
+        self.far(chunk)
+        self.near(chunk)
+
+    def far(self, chunk):
         for i in range(1, self.nf):
             self.copy(self.me, chunk, self.at(i, 0), self.send_f).start()
         for j in range(1, self.ns):
             self.copy(self.me, chunk, self.at(0, j), self.send_s).start()
+
+    def near(self, chunk):
         self.copy(self.me, chunk, self.sibling, self.send_b).start()
 
     def first(self, chunk):
@@ -74,9 +80,9 @@
                     device_id={"blk": self.sibling}, device_id_type=pl.DeviceIdType.MESH).wait_send()
 
 
-def kernel(nb, nw, total_walkers, chunks, flat, three, inv, rot_hbm, full_hbm, noise,
+def kernel(nb, nw, total_walkers, chunks, split, flat, three, inv, rot_hbm, full_hbm, noise,
            out, fb, shift,
-           rot, full, theta, acc, field, mid, outer_in, inner_in, slots_w, slots_b, current, total,
+           pair, mine, zout, zin, pin, rot, full, theta, acc, field, mid, outer_in, inner_in, slots_w, slots_b, current, total,
            rot_recv, rot_f, rot_s, rot_b, fld_recv, fld_f, fld_s, fld_b,
            load, slot_send, slot_recv, in_send, in_recv, mid_send, mid_recv, out_send, out_recv):
     blk, walk = lax.axis_index("blk"), lax.axis_index("walk")
@@ -100,71 +106,93 @@
 
     vectors = Gather(nb, per, lambda block, c: rot.at[block * per + c], lambda k: rot.at[pl.ds(0, k * per)],
                      rot_recv, rot_f, rot_s, rot_b)
+    vectors.far(0)
     for c in range(per):
-        vectors.own(c)
-
+        vectors.near(c)
+
+    def share(slots, source, me, peers, k):
+        for peer, slot in peers:
+            pltpu.make_async_remote_copy(
+                src_ref=slots.at[me] if source is None else source.at[slot], dst_ref=slots.at[me],
+                send_sem=slot_send.at[k], recv_sem=slot_recv.at[k], device_id=peer, device_id_type=MESH).start()
+
+        def finish():
+            rest = slots.at[pl.ds(0, len(peers))]
+            pltpu.make_async_remote_copy(
+                src_ref=rest, dst_ref=rest, send_sem=slot_send.at[k], recv_sem=slot_recv.at[k],
+                device_id=peers[0][0], device_id_type=MESH).wait()
+
+        return finish
+
+    walk_peers = [({"walk": (walk + d) % nw}, (walk + d) % nw) for d in range(1, nw)]
+    blk_peers = [({"blk": (blk + d) % nb}, (blk + d) % nb) for d in range(1, nb)]
     tile = 512
-    for w in range(wdev):
-        for lo in range(0, orbitals, tile):
-            theta[w, :, lo:lo + tile] = jnp.dot(inv[w], three[w, :, lo:lo + tile], preferred_element_type=f32).astype(bf16)
-
-    def bias(g):
-        for lo in range(0, orbitals, 256):
-            vector = rot[g, :, lo:lo + 256].astype(f32)
+    parts, span_width = (2, pair.shape[-1]) if split else (1, orbitals)
+
+    def project(begin, into):
+        for lo in range(0, span_width, tile):
+            span = pl.ds(pl.multiple_of(begin + lo, tile), tile)
+            both = jnp.zeros((occupied, tile), f32)
             for w in range(wdev):
-                product = vector * theta[w, :, lo:lo + 256].astype(f32)
-                acc[pl.ds(w * group + g, 1), lo:lo + 256] = jnp.sum(product, axis=0, keepdims=True)
-
-    def bias_block(block):
-        @pl.loop(0, per)
-        def _(c):
-            bias(block * per + c)
-
-    bias_block(blk)
-    for c in range(per):
-        vectors.first(c)
-    for i in range(1, vectors.nf):
-        bias_block(vectors.at(i, 0))
+                one = jnp.dot(inv[w], three[w, :, span], preferred_element_type=f32).astype(bf16)
+                theta[w, :, span] = one
+                both = both + one.astype(f32)
+            into[:, lo:lo + tile] = both
+
+    first_column = 0
+    if split:
+        project((1 - vectors.core) * span_width, pair.at[0])
+        swap = pltpu.make_async_remote_copy(
+            src_ref=pair.at[0], dst_ref=pair.at[1], send_sem=slot_send.at[4], recv_sem=slot_recv.at[4],
+            device_id={"blk": vectors.sibling}, device_id_type=MESH)
+        swap.start()
+        first_column = vectors.core * span_width
+        project(first_column, mine)
+        swap.wait()
+    else:
+        project(0, mine)
+    width = span_width // nw
+    for k in range(nw):
+        value = mine[:, k * width:(k + 1) * width]
+        if split:
+            value = value + pair[1, :, k * width:(k + 1) * width]
+        zout[k] = value.astype(bf16)
+    zin[pl.ds(walk, 1)] = zout[pl.ds(walk, 1)]
+    share(zin, zout, walk, walk_peers, 2)()
+    value = zin[0].astype(f32)
+    for k in range(1, nw):
+        value = value + zin[k].astype(f32)
+    if split:
+        place = blk // 2
+        plane_peers = [({"blk": (blk + 2 * d) % nb}, 0) for d in range(1, nb // 2)]
+    else:
+        place, plane_peers = blk, blk_peers
+    pin[pl.ds(place, 1)] = value.astype(bf16)[None]
+    finish = share(pin, None, place, plane_peers, 3)
+    for c in range(1, per):
+        vectors.far(c)
     for c in range(per):
         vectors.landed(vectors.sibling, c)
-    bias_block(vectors.sibling)
-    for c in range(per):
-        vectors.second(c)
-    for j in range(1, vectors.ns):
-        for i in range(vectors.nf):
-            bias_block(vectors.at(i, j))
-
-    @pl.loop(1, nb // 2)
-    def _(d):
-        block = (vectors.sibling + 2 * d) % nb
-        for c in range(per):
-            vectors.landed(block, c)
-        bias_block(block)
-
-    biases = jnp.sum(acc[...], axis=1, keepdims=True)
-    fb[...] = jnp.broadcast_to(biases, fb.shape)
-    part = biases[0:group]
-    for w in range(1, wdev):
-        part = part + biases[w * group:(w + 1) * group]
-    diagonal = lax.broadcasted_iota(jnp.int32, (group, 128), 0) == lax.broadcasted_iota(jnp.int32, (group, 128), 1)
-    line = jnp.sum(jnp.where(diagonal, jnp.broadcast_to(part, (group, 128)), 0.0), axis=0, keepdims=True)
-    for axis, count, me, slots, k in (("walk", nw, walk, slots_w, 0), ("blk", nb, blk, slots_b, 1)):
+    finish()
+    value = pin[0].astype(f32)
+    for k in range(1, pin.shape[0]):
+        value = value + pin[k].astype(f32)
+    columns = pl.ds(pl.multiple_of(first_column + walk * width, width), width)
+    spot = lax.broadcasted_iota(jnp.int32, (1, 128), 1)
+    line = jnp.zeros((1, 128), f32)
+    for c in range(per * parts):
+        g = place * per * parts + c
+        product = rot[g, :, columns].astype(f32) * value
+        one = jnp.sum(jnp.sum(product, axis=0, keepdims=True), axis=1, keepdims=True)
+        line = line + jnp.where(spot == g, one, 0.0)
+    for peers, me, slots, k in ((walk_peers, walk, slots_w, 0), (blk_peers, blk, slots_b, 1)):
         slots[pl.ds(me, 1)] = line[None]
-        if count > 1:
-            for d in range(1, count):
-                pltpu.make_async_remote_copy(
-                    src_ref=slots.at[me], dst_ref=slots.at[me], send_sem=slot_send.at[k], recv_sem=slot_recv.at[k],
-                    device_id={axis: (me + d) % count}, device_id_type=MESH).start()
-            rest = slots.at[pl.ds(0, count - 1)]
-            every = pltpu.make_async_remote_copy(
-                src_ref=rest, dst_ref=rest, send_sem=slot_send.at[k], recv_sem=slot_recv.at[k],
-                device_id={axis: (me + 1) % count}, device_id_type=MESH)
-            every.wait()
+        share(slots, None, me, peers, k)()
         line = slots[0]
-        for d in range(1, count):
+        for d in range(1, slots.shape[0]):
             line = line + slots[d]
     shifts = line / math.sqrt(total_walkers)
-    shift[...] = shifts
+    shift[...] = shifts[:, 0:group]
     shifted = (noise[...] - shifts[:, 0:group]) * time_root
     lane = lax.broadcasted_iota(jnp.int32, (1, group), 1)
     weights = [jnp.sum(jnp.where(lane == walk * local_count + j, shifted, 0.0), axis=1, keepdims=True)
@@ -243,12 +271,57 @@
         def _():
             action(c)
 
+    def bias(g):
+        for lo in range(0, orbitals, 256):
+            vector = rot[g, :, lo:lo + 256].astype(f32)
+            for w in range(wdev):
+                product = vector * theta[w, :, lo:lo + 256].astype(f32)
+                acc[pl.ds(w * group + g, 1), lo:lo + 256] = jnp.sum(product, axis=0, keepdims=True)
+
+    def bias_block(block):
+        @pl.loop(0, per)
+        def _(c):
+            bias(block * per + c)
+
+    def vectors_first():
+        bias_block(blk)
+        bias_block(vectors.sibling)
+        for i in range(1, vectors.nf):
+            bias_block(vectors.at(i, 0))
+
+    def vectors_second():
+        for c in range(per):
+            vectors.second(c)
+        for j in range(1, vectors.ns):
+            for i in range(vectors.nf):
+                bias_block(vectors.at(i, j))
+
+    def vectors_third():
+        @pl.loop(1, nb // 2)
+        def _(d):
+            block = (vectors.sibling + 2 * d) % nb
+            for c in range(per):
+                vectors.landed(block, c)
+            bias_block(block)
+
+    for c in range(per):
+        vectors.first(c)
+
     @pl.loop(0, chunks + 5)
     def _(t):
         when_chunk(t, reduce_in)
         when_chunk(t - lag, spread)
         when_chunk(t - lag - 1, gather.first)
         when_chunk(t - lag - 2, gather.second)
+        pl.when(t == lag)(vectors_first)
+        pl.when(t == lag + 2)(vectors_second)
+        pl.when(t == lag + 4)(vectors_third)
+
+    biases = jnp.sum(acc[...], axis=1, keepdims=True)
+    diagonal = lax.broadcasted_iota(jnp.int32, (group, group), 0) == lax.broadcasted_iota(jnp.int32, (group, group), 1)
+    for w in range(wdev):
+        column = jnp.broadcast_to(biases[w * group:(w + 1) * group], (group, group))
+        fb[w:w + 1, :] = jnp.sum(jnp.where(diagonal, column, 0.0), axis=0, keepdims=True)
 
     @pl.loop(0, nb // 2)
     def _(d):
@@ -300,17 +373,24 @@
     local_count, block_rows, _ = full_chol.shape
     chunks = 8
     size = block_rows // chunks
+    split = orbitals // 2 // nw % 128 == 0
+    half = orbitals // 2 if split else orbitals
     flat = walkers.reshape(wdev * double_rows, orbitals)
     inv = inv_intersection.transpose(0, 2, 1, 3).reshape(wdev, occupied, double_rows)
     vmem, hbm = pl.BlockSpec(memory_space=pltpu.VMEM), pl.BlockSpec(memory_space=pl.ANY)
     dma = pltpu.SemaphoreType.DMA
     out, fb, shift = pl.pallas_call(
-        functools.partial(kernel, nb, nw, wdev * nb * nw, chunks),
-        out_shape=(jax.ShapeDtypeStruct(flat.shape, bf16), jax.ShapeDtypeStruct((wdev * group, 128), f32),
-                   jax.ShapeDtypeStruct((1, 128), f32)),
+        functools.partial(kernel, nb, nw, wdev * nb * nw, chunks, split),
+        out_shape=(jax.ShapeDtypeStruct(flat.shape, bf16), jax.ShapeDtypeStruct((wdev, group), f32),
+                   jax.ShapeDtypeStruct((1, group), f32)),
         in_specs=[vmem, vmem, vmem, hbm, hbm, vmem],
         out_specs=(vmem, vmem, vmem),
         scratch_shapes=[
+            pltpu.VMEM((2, occupied, half), f32),
+            pltpu.VMEM((occupied, half), f32),
+            pltpu.VMEM((nw, occupied, half // nw), bf16),
+            pltpu.VMEM((nw, occupied, half // nw), bf16),
+            pltpu.VMEM((nb // 2 if split else nb, occupied, half // nw), bf16),
             pltpu.VMEM((group, occupied, orbitals), bf16),
             pltpu.VMEM(full_chol.shape, bf16),
             pltpu.VMEM((wdev, occupied, orbitals), bf16),
@@ -325,12 +405,12 @@
             pltpu.VMEM(flat.shape, f32),
             dma((nb, per)), dma, dma, dma,
             dma((nb, chunks)), dma, dma, dma,
-            dma((2,)), dma((2,)), dma((2,)),
+            dma((2,)), dma((5,)), dma((5,)),
             dma((chunks,)), dma((chunks,)), dma((chunks,)), dma((chunks,)), dma((chunks,)), dma((chunks,)),
         ],
         compiler_params=pltpu.CompilerParams(collective_id=0, has_side_effects=True, vmem_limit_bytes=60 * 2**20),
     )(flat, walkers, inv, rotated_chol, full_chol, field_noise.reshape(1, group))
-    return (out.reshape(walkers.shape), fb[:, 0].reshape(wdev, group), shift[0, :group])
+    return (out.reshape(walkers.shape), fb, shift.reshape(group))
 
 
 def solution(mesh):

time: 127 us -> 112 us (0.88)
  Pallas kernels: 117 us -> 103 us
  local copies, waits for them, and re-layouts: 9.36 us -> 7.84 us
    pallas_call x1, Pallas kernels: 117 us -> 103 us  [local(): pl.pallas_call(functools.partial(kernel, nb, nw, wdev * nb * nw, chunks,...]
    unnamed x2 -> x8, local copies, waits for them, and re-layouts: 5.09 us -> 6.17 us
where the time goes in v2:
time: 112 us
  Pallas kernels  103 us (92%)
  local copies, waits for them, and re-layouts  7.84 us (7%)
    pallas_call x1, Pallas kernels, local(): pl.pallas_call(functools.partial(kernel, nb, nw, wdev * nb * nw, chunks,...  103 us
    unnamed x8, local copies, waits for them, and re-layouts  6.17 us

profile of v2, /device:TPU:1, one launch (start us, length us, event | category | flops | bytes accessed | tf_op | source)
XLA Modules:
  0.0 112.0 jit_solution(3500205255534783142)
XLA Ops:
  0.6 1.7 %reshape.26.inv = bf16[2,100,200]{2,1,0:T(8,128)(2,1)} reshape(bf16[2,100,2,100]{3,2,1,0:T(2,128)(2,1)} %bitcast.7) | data formatting | bytes 160000 | tf_op jit(solution)/shard_map/reshape | solution.py:379
  2.3 2.3 %copy.11.rot_hbm = bf16[2,100,2048]{2,1,0:T(8,128)(2,1)} copy(bf16[2,100,2048]{2,0,1:T(2,128)(2,1)} %param.7) | data formatting | bytes 1638400 | tf_op args[2]
  4.6 103.5 %shard_map.76 = (bf16[400,2048]{1,0:T(8,128)(2,1)}, f32[2,16]{1,0:T(2,128)}, f32[1,16]{1,0:T(1,128)}) custom-call(bf16[400,2048]{1,0:T(8,128)(2,1)} %bitcast.5, bf16[2,200,2048]{2,1,0:T(8,128)(2,1)} %three.1, bf16[2,100,200]{2,1,0:T(8,128)(2,1)} %reshape.26.inv, bf16[2,100,2048]{2,1,0:T(8,128)(2,1)} %copy.11.rot_hbm, bf16[4,256,2048]{2,1,0:T(8,128)(2,1)} %full_hbm.1, ...), custom_call_target="tpu_custom_call" | custom-call | tf_op jit(solution)/shard_map/pallas_call | solution.py:382
  108.1 0.0 copy-start
  108.1 0.0 copy-start.1
  108.1 2.8 %copy.16 = bf16[2,200,2048]{2,1,0:T(8,128)(2,1)} copy(bf16[2,200,2048]{2,1,0:T(8,128)(2,1)} %bitcast.6) | data formatting | bytes 3276800
  110.9 0.0 copy-done
  110.9 0.6 copy.17
  111.4 0.0 copy-done.1
  111.4 0.5 copy.18
Async XLA Ops:
  108.1 2.8 %copy-start = (f32[2,16]{1,0:T(2,128)S(1)}, f32[2,16]{1,0:T(2,128)}, u32[]{:S(2)}) copy-start(f32[2,16]{1,0:T(2,128)} %get-tuple-element.13) | copy-start | bytes 388
  108.1 3.4 %copy-start.1 = (f32[1,16]{1,0:T(1,128)S(1)}, f32[1,16]{1,0:T(1,128)}, u32[]{:S(2)}) copy-start(f32[1,16]{1,0:T(1,128)} %get-tuple-element.8) | copy-start | bytes 196

commit v3 on v2

--- a/solution.py
+++ b/solution.py
@@ -82,14 +82,14 @@
 
 def kernel(nb, nw, total_walkers, chunks, split, flat, three, inv, rot_hbm, full_hbm, noise,
            out, fb, shift,
-           pair, mine, zout, zin, pin, rot, full, theta, acc, field, mid, outer_in, inner_in, slots_w, slots_b, current, total,
+           pair, mine, zout, zin, pin, rot, full, theta, acc, field, mid, outer_in, inner_in, slots_w, slots_b, terms,
            rot_recv, rot_f, rot_s, rot_b, fld_recv, fld_f, fld_s, fld_b,
            load, slot_send, slot_recv, in_send, in_recv, mid_send, mid_recv, out_send, out_recv):
     blk, walk = lax.axis_index("blk"), lax.axis_index("walk")
     wdev, occupied, orbitals = theta.shape
     per, group = rot_hbm.shape[0], rot.shape[0]
     local_count, block_rows = full_hbm.shape[0], full_hbm.shape[1]
-    size = block_rows // chunks
+    size = orbitals // chunks
     MESH = pl.DeviceIdType.MESH
 
     load_rot = pltpu.make_async_copy(rot_hbm, rot.at[pl.ds(blk * per, per)], load.at[0])
@@ -207,8 +207,10 @@
     inward = (walk + step + nw) % nw
     outward = (walk - step + nw) % nw
     lag = jnp.where(is_mid, 1, 3)
-    rows = lambda block, c: field.at[pl.ds(pl.multiple_of(block * block_rows + c * size, size), size)]
-    gather = Gather(nb, chunks, rows, lambda k: field.at[pl.ds(0, k * block_rows)], fld_recv, fld_f, fld_s, fld_b)
+    cols = lambda c: pl.ds(pl.multiple_of(c * size, size), size)
+    rows = lambda block: pl.ds(pl.multiple_of(block * block_rows, block_rows), block_rows)
+    part_at = lambda block, c: field.at[rows(block), cols(c)]
+    gather = Gather(nb, chunks, part_at, lambda k: field.at[pl.ds(0, k * block_rows)], fld_recv, fld_f, fld_s, fld_b)
 
     def hop(src, dst, send, recv, target):
         return pltpu.make_async_remote_copy(src_ref=src, dst_ref=dst, send_sem=send, recv_sem=recv,
@@ -221,15 +223,13 @@
         return hop(mid.at[c], inner_in.at[c], mid_send.at[c], mid_recv.at[c], inward)
 
     def back(c):
-        return hop(rows(blk, c), rows(blk, c), out_send.at[c], out_recv.at[c], outward)
+        return hop(part_at(blk, c), part_at(blk, c), out_send.at[c], out_recv.at[c], outward)
 
     def reduce_in(c):
-        span = pl.ds(pl.multiple_of(c * size, size), size)
-
         def summed():
-            value = weights[0] * full[0, span, :].astype(f32)
+            value = weights[0] * full[0, :, cols(c)].astype(f32)
             for j in range(1, local_count):
-                value = value + weights[j] * full[j, span, :].astype(f32)
+                value = value + weights[j] * full[j, :, cols(c)].astype(f32)
             return value
 
         @pl.when(has_outer)
@@ -253,8 +253,7 @@
         @pl.when(is_mid)
         def _():
             across(c).wait_recv()
-            span = pl.ds(pl.multiple_of(blk * block_rows + c * size, size), size)
-            field[span, :] = (mid[c].astype(f32) + inner_in[c].astype(f32)).astype(bf16)
+            field[rows(blk), cols(c)] = (mid[c].astype(f32) + inner_in[c].astype(f32)).astype(bf16)
 
         @pl.when(jnp.logical_not(is_mid))
         def _():
@@ -307,12 +306,18 @@
     for c in range(per):
         vectors.first(c)
 
-    @pl.loop(0, chunks + 5)
+    def first_term(c):
+        for d in range(nb // 2):
+            gather.landed((gather.sibling + 2 * d) % nb, c)
+        terms[0, :, cols(c)] = jnp.dot(flat[...], field[:, cols(c)], preferred_element_type=f32).astype(bf16)
+
+    @pl.loop(0, chunks + 6)
     def _(t):
         when_chunk(t, reduce_in)
         when_chunk(t - lag, spread)
         when_chunk(t - lag - 1, gather.first)
         when_chunk(t - lag - 2, gather.second)
+        when_chunk(t - lag - 3, first_term)
         pl.when(t == lag)(vectors_first)
         pl.when(t == lag + 2)(vectors_second)
         pl.when(t == lag + 4)(vectors_third)
@@ -323,29 +328,19 @@
         column = jnp.broadcast_to(biases[w * group:(w + 1) * group], (group, group))
         fb[w:w + 1, :] = jnp.sum(jnp.where(diagonal, column, 0.0), axis=0, keepdims=True)
 
-    @pl.loop(0, nb // 2)
-    def _(d):
-        @pl.loop(0, chunks)
-        def _(c):
-            gather.landed((gather.sibling + 2 * d) % nb, c)
-
-    source = flat
-    for order in range(1, orders + 1):
-        target = current.at[order % 2]
-
+    tile = orbitals // 2
+    for order in range(2, orders + 1):
         @pl.loop(0, orbitals // tile)
         def _(n):
             span = pl.ds(pl.multiple_of(n * tile, tile), tile)
-            term = (jnp.dot(source[...], field[:, span], preferred_element_type=f32) / order).astype(bf16)
-            before = flat[:, span].astype(f32) if order == 1 else total[:, span]
-            after = before + term.astype(f32)
+            term = (jnp.dot(terms[order - 2], field[:, span], preferred_element_type=f32) / order).astype(bf16)
             if order == orders:
-                out[:, span] = after.astype(bf16)
+                value = flat[:, span].astype(f32)
+                for k in range(orders - 1):
+                    value = value + terms[k, :, span].astype(f32)
+                out[:, span] = (value + term.astype(f32)).astype(bf16)
             else:
-                target[:, span] = term
-                total[:, span] = after
-
-        source = target
+                terms[order - 1, :, span] = term
 
     vectors.drain()
     gather.drain()
@@ -372,7 +367,7 @@
     per = rotated_chol.shape[0]
     local_count, block_rows, _ = full_chol.shape
     chunks = 8
-    size = block_rows // chunks
+    size = orbitals // chunks
     split = orbitals // 2 // nw % 128 == 0
     half = orbitals // 2 if split else orbitals
     flat = walkers.reshape(wdev * double_rows, orbitals)
@@ -396,13 +391,12 @@
             pltpu.VMEM((wdev, occupied, orbitals), bf16),
             pltpu.VMEM((wdev * group, orbitals), f32),
             pltpu.VMEM((orbitals, orbitals), bf16),
-            pltpu.VMEM((chunks, size, orbitals), bf16),
-            pltpu.VMEM((chunks, size, orbitals), bf16),
-            pltpu.VMEM((chunks, size, orbitals), bf16),
+            pltpu.VMEM((chunks, block_rows, size), bf16),
+            pltpu.VMEM((chunks, block_rows, size), bf16),
+            pltpu.VMEM((chunks, block_rows, size), bf16),
             pltpu.VMEM((nw, 1, 128), f32),
             pltpu.VMEM((nb, 1, 128), f32),
-            pltpu.VMEM((2,) + flat.shape, bf16),
-            pltpu.VMEM(flat.shape, f32),
+            pltpu.VMEM((orders - 1,) + flat.shape, bf16),
             dma((nb, per)), dma, dma, dma,
             dma((nb, chunks)), dma, dma, dma,
             dma((2,)), dma((5,)), dma((5,)),

time: 112 us -> 108 us (0.964)
  Pallas kernels: 103 us -> 98.8 us
    pallas_call x1, Pallas kernels: 103 us -> 98.8 us  [local(): pl.pallas_call(functools.partial(kernel, nb, nw, wdev * nb * nw, chunks,...]
where the time goes in v3:
time: 108 us; the launch traced here: 107 us
  Pallas kernels  98.8 us (91%)
  local copies, waits for them, and re-layouts  7.84 us (7%)
    pallas_call x1, Pallas kernels, local(): pl.pallas_call(functools.partial(kernel, nb, nw, wdev * nb * nw, chunks,...  98.8 us
    unnamed x8, local copies, waits for them, and re-layouts  6.17 us

profile of v3, /device:TPU:1, one launch (start us, length us, event | category | flops | bytes accessed | tf_op | source)
XLA Modules:
  0.0 107.3 jit_solution(778215289875429918)
XLA Ops:
  0.6 1.7 %reshape.26.inv = bf16[2,100,200]{2,1,0:T(8,128)(2,1)} reshape(bf16[2,100,2,100]{3,2,1,0:T(2,128)(2,1)} %bitcast.7) | data formatting | bytes 160000 | tf_op jit(solution)/shard_map/reshape | solution.py:374
  2.3 2.3 %copy.11.rot_hbm = bf16[2,100,2048]{2,1,0:T(8,128)(2,1)} copy(bf16[2,100,2048]{2,0,1:T(2,128)(2,1)} %param.7) | data formatting | bytes 1638400 | tf_op args[2]
  4.6 98.8 %shard_map.76 = (bf16[400,2048]{1,0:T(8,128)(2,1)}, f32[2,16]{1,0:T(2,128)}, f32[1,16]{1,0:T(1,128)}) custom-call(bf16[400,2048]{1,0:T(8,128)(2,1)} %bitcast.5, bf16[2,200,2048]{2,1,0:T(8,128)(2,1)} %three.1, bf16[2,100,200]{2,1,0:T(8,128)(2,1)} %reshape.26.inv, bf16[2,100,2048]{2,1,0:T(8,128)(2,1)} %copy.11.rot_hbm, bf16[4,256,2048]{2,1,0:T(8,128)(2,1)} %full_hbm.1, ...), custom_call_target="tpu_custom_call" | custom-call | tf_op jit(solution)/shard_map/pallas_call | solution.py:377
  103.4 0.0 copy-start
  103.4 0.0 copy-start.1
  103.4 2.8 %copy.16 = bf16[2,200,2048]{2,1,0:T(8,128)(2,1)} copy(bf16[2,200,2048]{2,1,0:T(8,128)(2,1)} %bitcast.6) | data formatting | bytes 3276800
  106.2 0.0 copy-done
  106.2 0.6 copy.17
  106.8 0.0 copy-done.1
  106.8 0.5 copy.18
Async XLA Ops:
  103.4 2.8 %copy-start = (f32[2,16]{1,0:T(2,128)S(1)}, f32[2,16]{1,0:T(2,128)}, u32[]{:S(2)}) copy-start(f32[2,16]{1,0:T(2,128)} %get-tuple-element.13) | copy-start | bytes 388
  103.4 3.4 %copy-start.1 = (f32[1,16]{1,0:T(1,128)S(1)}, f32[1,16]{1,0:T(1,128)}, u32[]{:S(2)}) copy-start(f32[1,16]{1,0:T(1,128)} %get-tuple-element.8) | copy-start | bytes 196

commit v4 on v3

--- a/solution.py
+++ b/solution.py
@@ -206,7 +206,7 @@
     step = 1 - 2 * (walk >= half).astype(jnp.int32)
     inward = (walk + step + nw) % nw
     outward = (walk - step + nw) % nw
-    lag = jnp.where(is_mid, 1, 3)
+    lag = jnp.where(is_mid, 1, 4)
     cols = lambda c: pl.ds(pl.multiple_of(c * size, size), size)
     rows = lambda block: pl.ds(pl.multiple_of(block * block_rows, block_rows), block_rows)
     part_at = lambda block, c: field.at[rows(block), cols(c)]
@@ -311,7 +311,7 @@
             gather.landed((gather.sibling + 2 * d) % nb, c)
         terms[0, :, cols(c)] = jnp.dot(flat[...], field[:, cols(c)], preferred_element_type=f32).astype(bf16)
 
-    @pl.loop(0, chunks + 6)
+    @pl.loop(0, chunks + 7)
     def _(t):
         when_chunk(t, reduce_in)
         when_chunk(t - lag, spread)

time: 108 us -> 108 us (level)
  no operation moved by 1% of the time
where the time goes in v4:
time: 108 us; the launch traced here: 107 us
  Pallas kernels  98.8 us (91%)
  local copies, waits for them, and re-layouts  7.84 us (7%)
    pallas_call x1, Pallas kernels, local(): pl.pallas_call(functools.partial(kernel, nb, nw, wdev * nb * nw, chunks,...  98.8 us
    unnamed x8, local copies, waits for them, and re-layouts  6.17 us

profile of v4, /device:TPU:1, one launch (start us, length us, event | category | flops | bytes accessed | tf_op | source)
XLA Modules:
  0.0 107.3 jit_solution(749010762225937911)
XLA Ops:
  0.6 1.7 %reshape.26.inv = bf16[2,100,200]{2,1,0:T(8,128)(2,1)} reshape(bf16[2,100,2,100]{3,2,1,0:T(2,128)(2,1)} %bitcast.7) | data formatting | bytes 160000 | tf_op jit(solution)/shard_map/reshape | solution.py:374
  2.3 2.3 %copy.11.rot_hbm = bf16[2,100,2048]{2,1,0:T(8,128)(2,1)} copy(bf16[2,100,2048]{2,0,1:T(2,128)(2,1)} %param.7) | data formatting | bytes 1638400 | tf_op args[2]
  4.6 98.8 %shard_map.76 = (bf16[400,2048]{1,0:T(8,128)(2,1)}, f32[2,16]{1,0:T(2,128)}, f32[1,16]{1,0:T(1,128)}) custom-call(bf16[400,2048]{1,0:T(8,128)(2,1)} %bitcast.5, bf16[2,200,2048]{2,1,0:T(8,128)(2,1)} %three.1, bf16[2,100,200]{2,1,0:T(8,128)(2,1)} %reshape.26.inv, bf16[2,100,2048]{2,1,0:T(8,128)(2,1)} %copy.11.rot_hbm, bf16[4,256,2048]{2,1,0:T(8,128)(2,1)} %full_hbm.1, ...), custom_call_target="tpu_custom_call" | custom-call | tf_op jit(solution)/shard_map/pallas_call | solution.py:377
  103.4 0.0 copy-start
  103.4 0.0 copy-start.1
  103.4 2.8 %copy.16 = bf16[2,200,2048]{2,1,0:T(8,128)(2,1)} copy(bf16[2,200,2048]{2,1,0:T(8,128)(2,1)} %bitcast.6) | data formatting | bytes 3276800
  106.2 0.0 copy-done
  106.2 0.6 copy.17
  106.8 0.0 copy-done.1
  106.8 0.5 copy.18
Async XLA Ops:
  103.4 2.8 %copy-start = (f32[2,16]{1,0:T(2,128)S(1)}, f32[2,16]{1,0:T(2,128)}, u32[]{:S(2)}) copy-start(f32[2,16]{1,0:T(2,128)} %get-tuple-element.13) | copy-start | bytes 388
  103.4 3.4 %copy-start.1 = (f32[1,16]{1,0:T(1,128)S(1)}, f32[1,16]{1,0:T(1,128)}, u32[]{:S(2)}) copy-start(f32[1,16]{1,0:T(1,128)} %get-tuple-element.8) | copy-start | bytes 196
